TPU v7x, 512 devices: a whole 4x8x8 slice. The times are simulated.
512 devices in a mesh: seq: 64 (over z, y), head: 8 (over x, core).
Axes of the slice: x: 4, y: 8, z: 8, core: 2. Of those that a mesh axis runs over, the one named last changes fastest.
Arguments:
- queries: bfloat16 [9216, 8192], P('seq', 'head'), may hold values from -24 to 24
- key_matrix: bfloat16 [9216, 1024], P('seq', 'head'), may hold values from -4 to 4
- value_matrix: bfloat16 [9216, 1024], P('seq', 'head'), may hold values from -6 to 6
- query_feature_weight: bfloat16 [128, 4096], P(None, 'head'), may hold values from -0.5 to 0.5
- key_feature_weight: bfloat16 [128, 512], P(None, 'head'), may hold values from -0.5 to 0.5
Outputs:
- student_out: bfloat16 [9216, 8192], P('seq', 'head')
- query_map_grad: float32 [128, 4096], P(None, 'head')
- key_weight_gradient: float32 [128, 512], P(None, 'head')
- transfer_loss: float32 [], replicated
All inputs are finite; a program needn't handle non-finite values.
Results may differ from a plain program's by a relative error of at most 0.008.
Values may be sent and summed in bfloat16 or wider, within the bound.
A program may use at most 128 MiB of HBM per device.

v0:
```python
import jax
import jax.numpy as jnp
from jax import lax
from jax.sharding import PartitionSpec as P

HEAD_SIZE = 128
GROUP_QUERIES = 8
HALF_FEATURES = 64
NEG_LARGE = -1e30


def prefix(shard, axis, join, neutral, backward):
    count = lax.axis_size(axis)
    place = lax.axis_index(axis)
    ahead = count - 1 - place if backward else place
    gathered = jax.tree.map(
        lambda a, kind: lax.all_gather(a.astype(kind), axis), shard, (jnp.bfloat16, jnp.bfloat16)
    )
    state = jax.tree.map(lambda a, e: jnp.zeros_like(a) + jnp.asarray(e, a.dtype), shard, neutral)

    def one(lap, state):
        source = count - 1 - lap if backward else lap
        return join(
            state,
            jax.tree.map(
                lambda a, own: lax.dynamic_index_in_dim(a, source, 0, False).astype(own.dtype),
                gathered,
                shard,
            ),
        )

    return lax.fori_loop(0, ahead, one, state)


def feature_pair(logits):
    plus_half = jax.nn.softmax(logits, axis=-1)
    minus_half = jax.nn.softmax(-logits, axis=-1)
    return (plus_half, minus_half)


def pair_backward(plus_half, minus_half, d_features):
    feat_count = plus_half.shape[-1]
    d_plus = d_features[..., :feat_count]
    d_minus = d_features[..., feat_count:]
    inner_plus = jnp.sum(d_plus * plus_half, axis=-1, keepdims=True)
    inner_minus = jnp.sum(d_minus * minus_half, axis=-1, keepdims=True)
    return plus_half * (d_plus - inner_plus) - minus_half * (d_minus - inner_minus)


def add_pair(earlier_pair, later_pair):
    return (earlier_pair[0] + later_pair[0], earlier_pair[1] + later_pair[1])


def attend(running, row_block, query_pos, key_view, value_view, key_pos, score_scale):
    row_max, row_sum, weighted = running
    scores = (
        jnp.einsum("rkgd,lkd->kgrl", row_block, key_view, preferred_element_type=jnp.float32)
        * score_scale
    )
    visible = key_pos[None, None, None, :] <= query_pos[None, None, :, None]
    masked = jnp.where(visible, scores, NEG_LARGE)
    new_max = jnp.maximum(row_max, jnp.max(masked, axis=-1))
    exponent = jnp.where(visible, jnp.exp(masked - new_max[..., None]), 0.0)
    weights = exponent.astype(jnp.bfloat16)
    weighted = jnp.einsum("kgrl,lkd->kgrd", weights, value_view, preferred_element_type=jnp.float32)
    row_sum = jnp.sum(exponent, axis=-1)
    return (new_max, row_sum, weighted)


def local(queries, key_matrix, value_matrix, query_feature_weight, key_feature_weight):
    token_rows = queries.shape[0]
    local_heads = key_matrix.shape[1] // HEAD_SIZE
    seq_count = lax.axis_size("seq")
    position = lax.axis_index("seq")
    first_row = position * token_rows
    seg_total = token_rows * seq_count
    score_scale = HEAD_SIZE ** (-0.5)
    query_heads = queries.reshape(token_rows, local_heads, GROUP_QUERIES, HEAD_SIZE)
    key_heads = key_matrix.reshape(token_rows, local_heads, HEAD_SIZE)
    value_heads = value_matrix.reshape(token_rows, local_heads, HEAD_SIZE)
    query_map_view = query_feature_weight.reshape(
        HEAD_SIZE, local_heads, GROUP_QUERIES, HALF_FEATURES
    )
    key_map_view = key_feature_weight.reshape(HEAD_SIZE, local_heads, HALF_FEATURES)
    query_sets = ((query_heads, first_row + jnp.arange(token_rows, dtype=jnp.int32)),)

    def fresh_carry(row_block):
        row_count = row_block.shape[0]
        return (
            jnp.full((local_heads, GROUP_QUERIES, row_count), NEG_LARGE, jnp.float32),
            jnp.zeros((local_heads, GROUP_QUERIES, row_count), jnp.float32),
            jnp.zeros((local_heads, GROUP_QUERIES, row_count, HEAD_SIZE), jnp.float32),
        )

    first_key = jnp.int32(0)
    key_block = lax.all_gather(key_matrix, "seq", axis=0, tiled=True)
    value_block = lax.all_gather(value_matrix, "seq", axis=0, tiled=True)
    key_count = key_block.shape[0]
    key_view = key_block.reshape(key_count, local_heads, HEAD_SIZE)
    value_view = value_block.reshape(key_count, local_heads, HEAD_SIZE)
    key_pos = jnp.arange(key_count, dtype=jnp.int32)
    teach_runs = tuple((fresh_carry(query_set[0]) for query_set in query_sets))
    updated = []
    for query_set, fold_teach_run in zip(query_sets, teach_runs):
        row_block, query_pos = query_set

        def visit_block(current, row_block=row_block, query_pos=query_pos):
            return attend(current, row_block, query_pos, key_view, value_view, key_pos, score_scale)

        def unchanged(current):
            return current

        updated.append(lax.cond(first_key <= query_pos[-1], visit_block, unchanged, fold_teach_run))
    teach_done = tuple(updated)

    def finish(teach_run):
        return (teach_run[2] / teach_run[1][..., None]).astype(jnp.bfloat16)

    finished = [finish(teach_run) for teach_run in teach_done]
    teacher = finished[0]
    query_logits = jnp.einsum(
        "tkgd,dkgf->kgtf", query_heads, query_map_view, preferred_element_type=jnp.float32
    )
    query_plus, query_minus = feature_pair(query_logits)
    query_phi = jnp.concatenate([query_plus, query_minus], axis=-1).astype(jnp.bfloat16)
    logits = jnp.einsum("lkd,dkf->klf", key_heads, key_map_view, preferred_element_type=jnp.float32)
    plus_half, minus_half = feature_pair(logits)
    key_phi = jnp.concatenate([plus_half, minus_half], axis=-1).astype(jnp.bfloat16)
    block_state = jnp.einsum(
        "ktf,tkd->kfd", key_phi, value_heads, preferred_element_type=jnp.float32
    )
    block_norm = jnp.sum(key_phi.astype(jnp.float32), axis=1)
    zero_pair = (jnp.zeros_like(block_state), jnp.zeros_like(block_norm))
    prefix_state, prefix_norm = prefix((block_state, block_norm), "seq", add_pair, zero_pair, False)
    prefix_low = prefix_state.astype(jnp.bfloat16)
    token_index = jnp.arange(token_rows, dtype=jnp.int32)
    causal = token_index[None, :] <= token_index[:, None]
    intra_scores = jnp.where(
        causal,
        jnp.einsum("kgtf,ksf->kgts", query_phi, key_phi, preferred_element_type=jnp.float32),
        0.0,
    )
    numerator = jnp.einsum(
        "kgts,skd->kgtd",
        intra_scores.astype(jnp.bfloat16),
        value_heads,
        preferred_element_type=jnp.float32,
    )
    numerator = numerator + jnp.einsum(
        "kgtf,kfd->kgtd", query_phi, prefix_low, preferred_element_type=jnp.float32
    )
    query_wide = query_phi.astype(jnp.float32)
    denominator = jnp.sum(intra_scores, axis=-1) + jnp.einsum(
        "kgtf,kf->kgt", query_wide, prefix_norm, precision=lax.Precision.HIGHEST
    )
    student = numerator / denominator[..., None]
    target = teacher.astype(jnp.float32)
    differ = student - target
    loss_local = jnp.sum(differ * differ)
    grad_out = 2.0 * differ / seg_total
    numer_grad = grad_out / denominator[..., None]
    denom_grad = -jnp.sum(grad_out * student, axis=-1) / denominator
    numer_low = numer_grad.astype(jnp.bfloat16)
    coupling = (
        jnp.einsum("kgtd,skd->kgts", numer_low, value_heads, preferred_element_type=jnp.float32)
        + denom_grad[..., None]
    )
    coupling_low = jnp.where(causal, coupling, 0.0).astype(jnp.bfloat16)
    later_state = jnp.einsum(
        "kgtf,kgtd->kfd", query_phi, numer_low, preferred_element_type=jnp.float32
    )
    later_norm = jnp.einsum("kgtf,kgt->kf", query_wide, denom_grad, precision=lax.Precision.HIGHEST)
    zero_later = (jnp.zeros_like(later_state), jnp.zeros_like(later_norm))
    suffix_state, suffix_norm = prefix((later_state, later_norm), "seq", add_pair, zero_later, True)
    suffix_low = suffix_state.astype(jnp.bfloat16)
    query_dphi = jnp.einsum(
        "kgts,ksf->kgtf", coupling_low, key_phi, preferred_element_type=jnp.float32
    )
    query_dphi = query_dphi + jnp.einsum(
        "kgtd,kfd->kgtf", numer_low, prefix_low, preferred_element_type=jnp.float32
    )
    query_dphi = query_dphi + denom_grad[..., None] * prefix_norm[:, None, None, :]
    key_dphi = jnp.einsum(
        "kgts,kgtf->ksf", coupling_low, query_phi, preferred_element_type=jnp.float32
    )
    key_dphi = key_dphi + jnp.einsum(
        "skd,kfd->ksf", value_heads, suffix_low, preferred_element_type=jnp.float32
    )
    key_dphi = key_dphi + suffix_norm[:, None, :]
    query_dlogit = pair_backward(query_plus, query_minus, query_dphi).astype(jnp.bfloat16)
    key_dlogit = pair_backward(plus_half, minus_half, key_dphi).astype(jnp.bfloat16)
    query_grad = jnp.einsum(
        "tkgd,kgtf->dkgf", query_heads, query_dlogit, preferred_element_type=jnp.float32
    )
    key_grad = jnp.einsum("tkd,ktf->dkf", key_heads, key_dlogit, preferred_element_type=jnp.float32)
    query_grad, key_grad = lax.psum((query_grad, key_grad), "seq")
    transfer_loss = lax.psum(loss_local, ("seq", "head")) / seg_total
    student_out = (
        student.astype(jnp.bfloat16)
        .transpose(2, 0, 1, 3)
        .reshape(token_rows, local_heads * GROUP_QUERIES * HEAD_SIZE)
    )
    return (
        student_out,
        query_grad.reshape(HEAD_SIZE, local_heads * GROUP_QUERIES * HALF_FEATURES),
        key_grad.reshape(HEAD_SIZE, local_heads * HALF_FEATURES),
        transfer_loss,
    )


def solution(mesh):
    placed = (
        P("seq", "head"),
        P("seq", "head"),
        P("seq", "head"),
        P(None, "head"),
        P(None, "head"),
    )
    return jax.shard_map(
        local,
        mesh=mesh,
        in_specs=placed,
        out_specs=(P("seq", "head"), P(None, "head"), P(None, "head"), P()),
        check_vma=False,
    )
```

profile of v0, /device:TPU:2, one launch (start us, length us, event | category | flops | bytes accessed | tf_op | source)
XLA Modules:
  0.0 812.8 jit_solution(13775298181172924217)
XLA Ops:
  7.9 0.9 fusion.99
  8.9 1.5 convolution_convert_fusion
  13.4 1.0 copy.51
  14.5 49.8 %all-gather.4 = bf16[64,1,128]{2,1,0:T(2,128)(2,1)S(1)} all-gather(bf16[1,1,128]{2,1,0:T(2,128)(2,1)S(1)} %bitcast.271), channel_id=3, replica_groups=mesh['seq'=64,'head'=8] {'seq'}, dimensions={0}, use_global_device_ids=true | all-gather | bytes 16640 | tf_op jit(solution)/shard_map/all_gather | solution.py:17
  64.3 1.3 fusion.103
  65.7 1.3 fusion.100
  67.5 1.1 fusion.38
  68.7 31.2 %all-gather.15.cloned.1.call-done = bf16[8192,128]{1,0:T(8,128)(2,1)} async-done(((bf16[128,128]{1,0:T(8,128)(2,1)}), bf16[8192,128]{1,0:T(8,128)(2,1)}) %all-gather.15.cloned.1.call-update) | async-done | bytes 2097168 | tf_op jit(solution)/shard_map/all_gather | solution.py:17
  100.2 83.5 %all-gather.11.cloned.1.call-done = bf16[9216,128]{1,0:T(8,128)(2,1)} async-done(((bf16[144,128]{1,0:T(8,128)(2,1)}), bf16[9216,128]{1,0:T(8,128)(2,1)}) %all-gather.11.cloned.1.call-update) | async-done | bytes 2359312 | tf_op jit(solution)/shard_map/all_gather | solution.py:96
  183.7 83.7 %all-gather.13.cloned.1.call-done = bf16[9216,128]{1,0:T(8,128)(2,1)} async-done(((bf16[144,128]{1,0:T(8,128)(2,1)}), bf16[9216,128]{1,0:T(8,128)(2,1)}) %all-gather.13.cloned.1.call-update) | async-done | bytes 2359312 | tf_op jit(solution)/shard_map/all_gather | solution.py:97
  267.4 62.5 %conditional.1 = (f32[1,8,144]{2,1,0:T(8,128)}, f32[1,8,144,128]{3,2,1,0:T(8,128)}) conditional(s32[]{:T(128)} %bitcast.28, () %tuple.33, (s32[9216]{0:T(1024)S(1)}, s32[144]{0:T(256)}, bf16[144,1024]{1,0:T(8,128)(2,1)}, bf16[9216,128]{1,0:T(8,128)(2,1)}, bf16[9216,128]{1,0:T(8,128)(2,1)}) %tuple.98), branch_computations={%region_12.13_spmd, %region_13.16_spmd} | conditional | flops 5575162880 | bytes 138378832 | solution.py:113
  267.6 1.4 broadcast_compare_fusion
  269.0 18.7 %fusion = (f32[8,144]{1,0:T(8,128)S(1)}, f32[9216,144,8]{0,1,2:T(8,128)}) fusion(pred[144,9216]{1,0:T(8,128)(4,1)S(1)} %broadcast_compare_fusion, bf16[9216,128]{1,0:T(8,128)(2,1)} %get-tuple-element.118, bf16[144,1024]{1,0:T(8,128)(2,1)} %get-tuple-element.119), kind=kOutput, calls=%fused_computation.4 | convolution fusion | flops 2749758464 | bytes 46453248 | tf_op jit(solution)/shard_map/cond/branch_1_fun/rkgd,lkd->kgrl/dot_general | solution.py:57
  287.7 21.9 %fusion.2 = f32[8,144]{1,0:T(8,128)} fusion(f32[9216,144,8]{0,1,2:T(8,128)} %get-tuple-element.217, f32[8,144]{1,0:T(8,128)S(1)} %broadcast_maximum_fusion, pred[144,9216]{1,0:T(8,128)(4,1)S(1)} %broadcast_compare_fusion), kind=kLoop, calls=%fused_computation.6 | loop fusion | flops 53083008 | bytes 43803648 | tf_op jit(solution)/shard_map/cond/branch_1_fun/reduce_sum | solution.py:66
  309.6 20.2 %fusion.10 = f32[1,8,144,128]{3,2,1,0:T(8,128)} fusion(bf16[9216,128]{1,0:T(8,128)(2,1)} %get-tuple-element.120, f32[9216,144,8]{0,1,2:T(8,128)} %get-tuple-element.217, f32[8,144]{1,0:T(8,128)S(1)} %broadcast_maximum_fusion, pred[144,9216]{1,0:T(8,128)(4,1)S(1)} %broadcast_compare_fusion), kind=kOutput, calls=%fused_computation.14 | convolution fusion | flops 2770993152 | bytes 46748160 | tf_op jit(solution)/shard_map/cond/branch_1_fun/kgrl,lkd->kgrd/dot_general | solution.py:65
  329.9 2.8 multiply_reduce_fusion
  332.9 1.9 fusion.34
  334.9 95.5 %psum.23 = f32[]{:T(128)} all-reduce(f32[]{:T(128)} %get-tuple-element.183), channel_id=1, replica_groups=mesh['seq'=64,'head'=8] {'seq','head'}, use_global_device_ids=true, to_apply=%region_26.27 | all-reduce | flops 1 | bytes 8 | tf_op jit(solution)/shard_map/psum | solution.py:197
  432.8 0.8 copy.65
  434.1 42.6 %all-gather.5 = bf16[64,1,128]{2,1,0:T(2,128)(2,1)S(1)} all-gather(bf16[1,1,128]{2,1,0:T(2,128)(2,1)S(1)} %fusion.36), channel_id=5, replica_groups=mesh['seq'=64,'head'=8] {'seq'}, dimensions={0}, use_global_device_ids=true | all-gather | bytes 16640 | tf_op jit(solution)/shard_map/all_gather | solution.py:17
  477.8 51.3 %while.27 = (s32[]{:T(128)}, f32[1,128,128]{2,1,0:T(8,128)S(1)}, f32[1,128]{1,0:T(1,128)S(1)}, s32[]{:T(128)}, bf16[64,1,128,128]{3,2,1,0:T(8,128)(2,1)}, /*inde...) while((s32[]{:T(128)}, f32[1,128,128]{2,1,0:T(8,128)S(1)}, ...), condition=%wide.region_21.22_spmd, body=%wide.region_20.21_spmd.sunk | while | flops 33030 | bytes 165283 | solution.py:32
  483.5 0.8 convert_add_fusion.10
  484.3 0.8 convert_add_fusion.10
  490.0 0.8 convert_add_fusion.10
  490.8 0.8 convert_add_fusion.10
  494.9 0.8 convert_add_fusion.10
  495.7 0.8 convert_add_fusion.10
  498.2 0.8 convert_add_fusion.10
  499.0 0.8 convert_add_fusion.10
  501.4 0.8 convert_add_fusion.10
  529.5 274.0 %psum.22 = f32[128,64]{0,1:T(8,128)} all-reduce(f32[128,64]{0,1:T(8,128)S(1)} %convolution_bitcast_fusion.3), channel_id=1, replica_groups=mesh['seq'=64,'head'=8] {'seq'}, use_global_device_ids=true, to_apply=%region_24.25 | all-reduce | flops 8192 | bytes 65536 | tf_op jit(solution)/shard_map/psum | solution.py:196
  803.5 1.7 copy.144
  (187 shorter events, 50.6 us)
Async XLA Ops:
  7.2 0.7 copy-start
  7.2 92.6 %all-gather.15.cloned.1.call-start = ((), (), s32[]{:S(2)}) async-start(), calls=%async_computation.3 | async-start | bytes 2129920 | tf_op jit(solution)/shard_map/all_gather | solution.py:17
  8.8 4.5 copy-start.5
  8.9 4.4 copy-start.7
  8.9 4.4 copy-start.9
  10.5 173.1 %all-gather.11.cloned.1.call-start = ((), (), s32[]{:S(2)}) async-start(), calls=%async_computation | async-start | bytes 2396160 | tf_op jit(solution)/shard_map/all_gather | solution.py:96
  11.3 256.1 %all-gather.13.cloned.1.call-start = ((), (), s32[]{:S(2)}) async-start(), calls=%async_computation.1 | async-start | bytes 2396160 | tf_op jit(solution)/shard_map/all_gather | solution.py:97
  12.0 465.7 %all-gather.17.cloned.1.call-start = ((), (), s32[]{:S(2)}) async-start(), calls=%async_computation.4 | async-start | bytes 2129920 | tf_op jit(solution)/shard_map/all_gather | solution.py:17
  12.1 1.3 copy-start.11
  67.1 200.2 %copy-start.2 = (bf16[8,144,64]{1,2,0:T(8,128)(2,1)}, bf16[8,144,64]{1,2,0:T(8,128)(2,1)S(1)}, u32[]{:S(2)}) copy-start(bf16[8,144,64]{1,2,0:T(8,128)(2,1)S(1)} %get-tuple-element.233) | copy-start | bytes 442372
  267.4 163.9 %copy-start.1 = (bf16[144,128]{1,0:T(8,128)(2,1)S(1)}, bf16[144,128]{1,0:T(8,128)(2,1)}, u32[]{:S(2)}) copy-start(bf16[144,128]{1,0:T(8,128)(2,1)} %param.13) | copy-start | bytes 110596
  329.9 102.6 %copy-start.12 = (bf16[144,1024]{1,0:T(8,128)(2,1)S(1)}, bf16[144,1024]{1,0:T(8,128)(2,1)}, u32[]{:S(2)}) copy-start(bf16[144,1024]{1,0:T(8,128)(2,1)} %param.11) | copy-start | bytes 884740
  329.9 103.8 %copy-start.3 = (bf16[8,144,64]{1,2,0:T(8,128)(2,1)S(1)}, bf16[8,144,64]{1,2,0:T(8,128)(2,1)}, u32[]{:S(2)}) copy-start(bf16[8,144,64]{1,2,0:T(8,128)(2,1)} %copy-done.2) | copy-start | bytes 442372
  332.7 196.6 %copy-start.6 = (f32[144]{0:T(256)S(1)}, f32[144]{0:T(256)}, u32[]{:S(2)}) copy-start(f32[144]{0:T(256)} %copy-done.5) | copy-start | bytes 1732
  332.7 196.6 %copy-start.8 = (f32[144]{0:T(256)S(1)}, f32[144]{0:T(256)}, u32[]{:S(2)}) copy-start(f32[144]{0:T(256)} %copy-done.7) | copy-start | bytes 1732
  332.7 196.6 %copy-start.10 = (f32[144]{0:T(256)S(1)}, f32[144]{0:T(256)}, u32[]{:S(2)}) copy-start(f32[144]{0:T(256)} %copy-done.9) | copy-start | bytes 1732
  332.9 196.5 %copy-start.4 = (bf16[144,128]{1,0:T(8,128)(2,1)S(1)}, bf16[144,128]{1,0:T(8,128)(2,1)}, u32[]{:S(2)}) copy-start(bf16[144,128]{1,0:T(8,128)(2,1)} %param.12) | copy-start | bytes 110596
  334.8 468.7 %all-reduce.2.cloned.1.call-start = ((), (), s32[]{:S(2)}) async-start(), calls=%async_computation.2 | async-start | bytes 524288 | tf_op jit(solution)/shard_map/psum | solution.py:196
Sparse Core Ops, SparseCore 0:
  11.6 88.1 all-gather.14
  102.9 80.7 all-gather.10
  186.7 80.5 all-gather.12
  334.9 80.1 all-gather.16
  477.2 147.5 all-reduce.1
where the time goes:
time: 818 us; the launch traced here: 813 us
  blocking collectives  462 us (56%)
  waiting for transfers between devices  200 us (24%)
  other arithmetic  73.9 us (9%)
  matrix products  53 us (6%)
  between operations  16.5 us (2%)
    psum x1, blocking collectives, local(): query_grad, key_grad = lax.psum((query_grad, key_grad), 'seq')  274 us
    psum x1, blocking collectives, local(): transfer_loss = lax.psum(loss_local, ('seq', 'head')) / seg_total  95.5 us
    all_gather x2, blocking collectives, prefix(): lax.all_gather(a.astype(kind), axis)  92.4 us
    all_gather x1, waiting for transfers between devices, local(): value_block = lax.all_gather(value_matrix, 'seq', axis=0, tiled=True)  83.7 us
    all_gather x1, waiting for transfers between devices, local(): key_block = lax.all_gather(key_matrix, 'seq', axis=0, tiled=True)  83.5 us
    add x126, other arithmetic, add_pair(): return (earlier_pair[0] + later_pair[0], earlier_pair[1] + later_pair[1])  49.7 us
    all_gather x2, waiting for transfers between devices, prefix(): lax.all_gather(a.astype(kind), axis)  31.2 us
    reduce_sum x1, other arithmetic, attend(): row_sum = jnp.sum(exponent, axis=-1)  21.9 us
  transfers between devices with their start and end apart: 5, of which 3 were waited for; matrix products, arithmetic and copies ran while one was open for 7% of the time, Pallas kernels for 0%

commit v1 on v0

--- a/solution.py
+++ b/solution.py
@@ -93,8 +93,10 @@
         )
 
     first_key = jnp.int32(0)
-    key_block = lax.all_gather(key_matrix, "seq", axis=0, tiled=True)
-    value_block = lax.all_gather(value_matrix, "seq", axis=0, tiled=True)
+    main = jnp.concatenate([key_matrix, value_matrix], axis=1)
+    key_block, value_block = jnp.split(
+        jax.lax.all_gather(main, axis_name="seq", axis=0, tiled=True), [key_matrix.shape[1]], axis=1
+    )
     key_count = key_block.shape[0]
     key_view = key_block.reshape(key_count, local_heads, HEAD_SIZE)
     value_view = value_block.reshape(key_count, local_heads, HEAD_SIZE)

time: 818 us -> 737 us (0.901)
  waiting for transfers between devices: 200 us -> 118 us
    all_gather x2 -> x1, waiting for transfers between devices: 167 us -> 87.2 us  [local(): jax.lax.all_gather(main, axis_name='seq', axis=0, tiled=True)]
  transfers between devices with their start and end apart: 5 -> 4, of which waited for: 3 -> 2; matrix products, arithmetic and copies ran while one was open for 7% -> 9% of each run, Pallas kernels for 0% -> 0%
where the time goes in v1:
time: 737 us; the launch traced here: 732 us
  blocking collectives  463 us (63%)
  waiting for transfers between devices  118 us (16%)
  other arithmetic  75.1 us (10%)
  matrix products  50.9 us (7%)
  between operations  16.5 us (2%)
    psum x1, blocking collectives, local(): query_grad, key_grad = lax.psum((query_grad, key_grad), 'seq')  274 us
    psum x1, blocking collectives, local(): transfer_loss = lax.psum(loss_local, ('seq', 'head')) / seg_total  95.5 us
    all_gather x2, blocking collectives, prefix(): lax.all_gather(a.astype(kind), axis)  93.2 us
    all_gather x1, waiting for transfers between devices, local(): jax.lax.all_gather(main, axis_name='seq', axis=0, tiled=True)  87.2 us
    add x126, other arithmetic, add_pair(): return (earlier_pair[0] + later_pair[0], earlier_pair[1] + later_pair[1])  49.8 us
    all_gather x2, waiting for transfers between devices, prefix(): lax.all_gather(a.astype(kind), axis)  31.1 us
    reduce_sum x1, other arithmetic, attend(): row_sum = jnp.sum(exponent, axis=-1)  21.5 us
    dot_general x1, matrix products, attend(): jnp.einsum('rkgd,lkd->kgrl', row_block, key_view, preferred_element_type=...  18.7 us
  transfers between devices with their start and end apart: 4, of which 2 were waited for; matrix products, arithmetic and copies ran while one was open for 9% of the time, Pallas kernels for 0%

profile of v1, /device:TPU:2, one launch (start us, length us, event | category | flops | bytes accessed | tf_op | source)
XLA Modules:
  0.0 731.8 jit_solution(14801025356595537953)
XLA Ops:
  7.9 0.9 fusion.101
  9.0 1.6 convolution_convert_fusion
  10.6 1.4 pad_maximum_fusion.1
  13.4 1.0 copy.51
  14.6 49.8 %all-gather.4 = bf16[64,1,128]{2,1,0:T(2,128)(2,1)S(1)} all-gather(bf16[1,1,128]{2,1,0:T(2,128)(2,1)S(1)} %bitcast.273), channel_id=3, replica_groups=mesh['seq'=64,'head'=8] {'seq'}, dimensions={0}, use_global_device_ids=true | all-gather | bytes 16640 | tf_op jit(solution)/shard_map/all_gather | solution.py:17
  64.4 1.3 fusion.105
  65.7 1.3 fusion.102
  67.6 1.1 fusion.40
  68.7 31.1 %all-gather.12.cloned.1.call-done = bf16[8192,128]{1,0:T(8,128)(2,1)} async-done(((bf16[128,128]{1,0:T(8,128)(2,1)}), bf16[8192,128]{1,0:T(8,128)(2,1)}) %all-gather.12.cloned.1.call-update) | async-done | bytes 2097168 | tf_op jit(solution)/shard_map/all_gather | solution.py:17
  100.2 87.2 %all-gather.10.cloned.1.call-done = bf16[9216,256]{1,0:T(8,128)(2,1)} async-done(((bf16[144,256]{1,0:T(8,128)(2,1)}), bf16[9216,256]{1,0:T(8,128)(2,1)}) %all-gather.10.cloned.1.call-update) | async-done | bytes 4718608 | tf_op jit(solution)/shard_map/all_gather | solution.py:98
  187.4 58.2 %conditional.1 = (f32[1,8,144]{2,1,0:T(8,128)S(1)}, f32[1,8,144,128]{3,2,1,0:T(8,128)S(1)}) conditional(s32[]{:T(128)} %bitcast.28, () %tuple.33, (s32[9216]{0:T(1024)S(1)}, s32[144]{0:T(256)S(1)}, bf16[9216,256]{1,0:T(8,128)(2,1)}, bf16[144,1024]{1,0:T(8,128)(2,1)}) %tuple.34), branch_computations={%region_12.13_spmd, %region_13.16_spmd} | conditional | flops 5575162880 | bytes 157256816 | solution.py:115
  188.4 18.7 %fusion = (f32[8,144]{1,0:T(8,128)S(1)}, f32[9216,144,8]{0,1,2:T(8,128)}) fusion(pred[144,9216]{1,0:T(8,128)(4,1)S(1)} %broadcast_compare_fusion, bf16[9216,256]{1,0:T(8,128)(2,1)} %get-tuple-element.119, bf16[144,1024]{1,0:T(8,128)(2,1)} %get-tuple-element.120), kind=kOutput, calls=%fused_computation.4 | convolution fusion | flops 2749758464 | bytes 46453248 | tf_op jit(solution)/shard_map/cond/branch_1_fun/rkgd,lkd->kgrl/dot_general | solution.py:57
  207.1 21.5 %fusion.2 = f32[8,144]{1,0:T(8,128)S(1)} fusion(f32[9216,144,8]{0,1,2:T(8,128)} %get-tuple-element.217, f32[8,144]{1,0:T(8,128)S(1)} %broadcast_maximum_fusion, pred[144,9216]{1,0:T(8,128)(4,1)S(1)} %broadcast_compare_fusion), kind=kLoop, calls=%fused_computation.6 | loop fusion | flops 53083008 | bytes 43803648 | tf_op jit(solution)/shard_map/cond/branch_1_fun/reduce_sum | solution.py:66
  228.7 17.0 %fusion.12 = f32[1,8,144,128]{3,2,1,0:T(8,128)S(1)} fusion(bf16[9216,256]{1,0:T(8,128)(2,1)S(1)} %copy-done.15, f32[9216,144,8]{0,1,2:T(8,128)} %get-tuple-element.217, f32[8,144]{1,0:T(8,128)S(1)} %broadcast_maximum_fusion, pred[144,9216]{1,0:T(8,128)(4,1)S(1)} %broadcast_compare_fusion), kind=kOutput, calls=%fused_computation.16 | convolution fusion | flops 2770993152 | bytes 46751744 | tf_op jit(solution)/shard_map/cond/branch_1_fun/kgrl,lkd->kgrd/dot_general | solution.py:65
  246.3 2.4 multiply_reduce_fusion
  248.9 0.9 fusion.36
  249.9 95.5 %psum.23 = f32[]{:T(128)} all-reduce(f32[]{:T(128)} %get-tuple-element.183), channel_id=1, replica_groups=mesh['seq'=64,'head'=8] {'seq','head'}, use_global_device_ids=true, to_apply=%region_26.27 | all-reduce | flops 1 | bytes 8 | tf_op jit(solution)/shard_map/psum | solution.py:199
  347.0 1.1 fusion.27
  348.4 1.1 fusion.26
  349.7 1.3 fusion.47
  351.0 0.8 copy.65
  352.3 43.4 %all-gather.5 = bf16[64,1,128]{2,1,0:T(2,128)(2,1)S(1)} all-gather(bf16[1,1,128]{2,1,0:T(2,128)(2,1)S(1)} %fusion.38), channel_id=5, replica_groups=mesh['seq'=64,'head'=8] {'seq'}, dimensions={0}, use_global_device_ids=true | all-gather | bytes 16640 | tf_op jit(solution)/shard_map/all_gather | solution.py:17
  396.8 51.3 %while.27 = (s32[]{:T(128)}, f32[1,128,128]{2,1,0:T(8,128)S(1)}, f32[1,128]{1,0:T(1,128)S(1)}, s32[]{:T(128)}, bf16[64,1,128,128]{3,2,1,0:T(8,128)(2,1)}, /*inde...) while((s32[]{:T(128)}, f32[1,128,128]{2,1,0:T(8,128)S(1)}, ...), condition=%wide.region_21.22_spmd, body=%wide.region_20.21_spmd.sunk | while | flops 33030 | bytes 165283 | solution.py:32
  402.5 0.8 convert_add_fusion.10
  403.3 0.8 convert_add_fusion.10
  409.0 0.8 convert_add_fusion.10
  409.8 0.8 convert_add_fusion.10
  413.1 0.8 convert_add_fusion.10
  413.9 0.8 convert_add_fusion.10
  414.7 0.8 convert_add_fusion.10
  448.5 274.0 %psum.22 = f32[128,64]{0,1:T(8,128)} all-reduce(f32[128,64]{0,1:T(8,128)S(1)} %convolution_bitcast_fusion.3), channel_id=1, replica_groups=mesh['seq'=64,'head'=8] {'seq'}, use_global_device_ids=true, to_apply=%region_24.25 | all-reduce | flops 8192 | bytes 65536 | tf_op jit(solution)/shard_map/psum | solution.py:198
  722.5 1.7 copy.144
  (191 shorter events, 51.9 us)
Async XLA Ops:
  7.2 0.7 copy-start
  7.2 92.6 %all-gather.12.cloned.1.call-start = ((), (), s32[]{:S(2)}) async-start(), calls=%async_computation.2 | async-start | bytes 2129920 | tf_op jit(solution)/shard_map/all_gather | solution.py:17
  8.8 4.5 copy-start.6
  8.8 4.5 copy-start.8
  8.9 4.5 copy-start.10
  8.9 4.5 copy-start.12
  9.0 90.9 %copy-start.4 = (bf16[144,64]{0,1:T(8,128)(2,1)}, bf16[144,64]{0,1:T(8,128)(2,1)S(1)}, u32[]{:S(2)}) copy-start(bf16[144,64]{0,1:T(8,128)(2,1)S(1)} %get-tuple-element.222) | copy-start | bytes 55300
  9.0 178.5 %copy-start.3 = (bf16[144,64]{0,1:T(8,128)(2,1)}, bf16[144,64]{0,1:T(8,128)(2,1)S(1)}, u32[]{:S(2)}) copy-start(bf16[144,64]{0,1:T(8,128)(2,1)S(1)} %get-tuple-element.219) | copy-start | bytes 55300
  10.6 176.9 %all-gather.10.cloned.1.call-start = ((), (), s32[]{:S(2)}) async-start(), calls=%async_computation | async-start | bytes 4792320 | tf_op jit(solution)/shard_map/all_gather | solution.py:98
  12.1 384.7 %all-gather.14.cloned.1.call-start = ((), (), s32[]{:S(2)}) async-start(), calls=%async_computation.3 | async-start | bytes 2129920 | tf_op jit(solution)/shard_map/all_gather | solution.py:17
  64.4 3.2 copy-start.5
  187.4 159.5 %copy-start.1 = (bf16[144,128]{1,0:T(8,128)(2,1)S(1)}, bf16[144,128]{1,0:T(8,128)(2,1)}, u32[]{:S(2)}) copy-start(bf16[144,128]{1,0:T(8,128)(2,1)} %param.13) | copy-start | bytes 110596
  207.1 21.5 %copy-start.15 = (bf16[9216,256]{1,0:T(8,128)(2,1)S(1)}, bf16[9216,256]{1,0:T(8,128)(2,1)}, u32[]{:S(2)}) copy-start(bf16[9216,256]{1,0:T(8,128)(2,1)} %get-tuple-element.119) | copy-start | bytes 14155780 | tf_op jit(solution)/shard_map/cond
  245.7 0.6 copy-start.14
  248.6 199.6 %copy-start.7 = (f32[144]{0:T(256)S(1)}, f32[144]{0:T(256)}, u32[]{:S(2)}) copy-start(f32[144]{0:T(256)} %copy-done.6) | copy-start | bytes 1732
  248.6 199.6 %copy-start.9 = (f32[144]{0:T(256)S(1)}, f32[144]{0:T(256)}, u32[]{:S(2)}) copy-start(f32[144]{0:T(256)} %copy-done.8) | copy-start | bytes 1732
  248.6 199.6 %copy-start.11 = (f32[144]{0:T(256)S(1)}, f32[144]{0:T(256)}, u32[]{:S(2)}) copy-start(f32[144]{0:T(256)} %copy-done.10) | copy-start | bytes 1732
  248.6 199.7 %copy-start.13 = (f32[144]{0:T(256)S(1)}, f32[144]{0:T(256)}, u32[]{:S(2)}) copy-start(f32[144]{0:T(256)} %copy-done.12) | copy-start | bytes 1732
  248.9 199.5 %copy-start.2 = (bf16[144,128]{1,0:T(8,128)(2,1)S(1)}, bf16[144,128]{1,0:T(8,128)(2,1)}, u32[]{:S(2)}) copy-start(bf16[144,128]{1,0:T(8,128)(2,1)} %param.12) | copy-start | bytes 110596
  249.8 472.6 %all-reduce.2.cloned.1.call-start = ((), (), s32[]{:S(2)}) async-start(), calls=%async_computation.1 | async-start | bytes 524288 | tf_op jit(solution)/shard_map/psum | solution.py:198
Sparse Core Ops, SparseCore 0:
  11.6 88.1 all-gather.11
  103.4 83.9 all-gather.9
  250.0 80.2 all-gather.13
  396.2 147.4 all-reduce.1
